TPU v7x, 32 devices: a whole 2x2x4 slice. The times are simulated.
32 devices in a mesh: groups: 2 (over y), img: 4 (over z), pair: 2 (over x), sub: 2 (over core).
Axes of the slice: x: 2, y: 2, z: 4, core: 2. Of those that a mesh axis runs over, the one named last changes fastest.
Arguments:
- descriptors: bfloat16 [16, 1024, 256], P(('groups', 'img', 'pair')), parts along dimension 0
- links: int32 [16, 3], P('groups'), parts along dimension 0, may hold values 0 or 1
- qk_weight: bfloat16 [256, 256], P(None, 'sub'), may hold values from -0.375 to 0.375
- value_weight: bfloat16 [256, 256], P(None, 'sub'), may hold values from -0.375 to 0.375
- out_weight: bfloat16 [256, 256], replicated, may hold values from -0.375 to 0.375
- mlp_in: bfloat16 [512, 512], replicated, may hold values from -0.25 to 0.25
- mlp_in_bias: float32 [512], replicated, may hold values from -4 to 4
- norm_gain: float32 [512], replicated, may hold values from 0.1 to 1.9
- norm_bias: float32 [512], replicated, may hold values from -3 to 3
- mlp_out: bfloat16 [512, 256], replicated, may hold values from -0.25 to 0.25
- mlp_out_bias: float32 [256], replicated, may hold values from -3 to 3
Outputs:
- updated: bfloat16 [16, 1024, 256], P(('groups', 'img', 'pair'), 'sub'), parts along dimension 0
There are 2 independent parts, one for each index of `groups`. A program takes and returns all parts, laid end to end along the dimension named above; an argument that names none is the same for every part. Nothing has to cross between parts.
All inputs are finite; a program needn't handle non-finite values.
Results may differ from a plain program's by a relative error of at most 0.0045.
Values may be sent and summed in bfloat16 or wider, within the bound.
No kernel may reach another device: no remote copies, remote signals or barrier semaphores. Data moves between devices by JAX's collectives and lax.ppermute only.
A program may use at most 64 MiB of HBM per device.

v0:
```python
import math
import jax
import jax.numpy as jnp
from jax import lax
from jax.sharding import PartitionSpec as P

D = 256
HEADS = 4
SPAN = 3


def passed_along(value, axis, by):
    length = lax.axis_size(axis)
    pairs = [(i, i + by) for i in range(length) if 0 <= i + by < length]
    return lax.ppermute(value, axis, pairs)


def link_value(links, lower_image, step_size, image_count):
    inside = jnp.logical_and(lower_image >= 0, lower_image + step_size < image_count)
    clipped = jnp.clip(lower_image, 0, image_count - 1)
    entry = lax.dynamic_slice(links, (clipped, jnp.int32(step_size - 1)), (1, 1))[0, 0]
    return jnp.where(inside, entry, 0).astype(jnp.float32)


def fetch_partner(offset, packed, local_width):
    partner = passed_along(packed, ("img", "pair"), -offset)
    return (partner[:, :local_width], partner[:, local_width:])


def tile_messages(own_keys, partner_keys, partner_values):
    head_width = D // HEADS
    score_scale = 1.0 / math.sqrt(head_width)
    heads_local = own_keys.shape[1] // head_width
    to_own = []
    for head_id in range(heads_local):
        lo_col = head_id * head_width
        query_part = own_keys[:, lo_col : lo_col + head_width]
        key_part = partner_keys[:, lo_col : lo_col + head_width]
        scores = (
            jnp.einsum("qd,kd->qk", query_part, key_part, preferred_element_type=jnp.float32)
            * score_scale
        )
        row_weights = jax.nn.softmax(scores, axis=1).astype(jnp.bfloat16)
        to_own.append(
            jnp.dot(
                row_weights,
                partner_values[:, lo_col : lo_col + head_width],
                preferred_element_type=jnp.float32,
            ).astype(jnp.bfloat16)
        )
    own_result = jnp.concatenate(to_own, axis=1)
    return (own_result, own_result)


def on_device(
    descriptors,
    links,
    qk_weight,
    value_weight,
    out_weight,
    mlp_in,
    mlp_in_bias,
    norm_gain,
    norm_bias,
    mlp_out,
    mlp_out_bias,
):
    own_rows = descriptors[0]
    key_rows = jnp.dot(own_rows, qk_weight, preferred_element_type=jnp.float32).astype(jnp.bfloat16)
    value_rows = jnp.dot(own_rows, value_weight, preferred_element_type=jnp.float32).astype(
        jnp.bfloat16
    )
    local_width = key_rows.shape[1]
    packed = jnp.concatenate([key_rows, value_rows], axis=1)
    half_rows = own_rows.shape[0] // lax.axis_size("sub")
    row_start = lax.axis_index("sub") * half_rows
    own_half = lax.dynamic_slice_in_dim(own_rows, row_start, half_rows, 0)
    position = lax.axis_index(("img", "pair"))
    image_count = lax.axis_size(("img", "pair"))
    summed = jnp.zeros(key_rows.shape, jnp.float32)
    offsets = list(range(1, SPAN + 1)) + list(range(-SPAN, 0))
    for offset in offsets:
        partner_keys, partner_values = fetch_partner(offset, packed, local_width)
        step_size = abs(offset)
        lower_image = position + min(offset, 0)
        linked = link_value(links, lower_image, step_size, image_count)
        message, unused = tile_messages(key_rows, partner_keys, partner_values)
        summed = summed + linked * message.astype(jnp.float32)
    summed_b = summed.astype(jnp.bfloat16)
    gathered = lax.all_to_all(summed_b, "sub", split_axis=0, concat_axis=1, tiled=True)
    projected = jnp.dot(gathered, out_weight, preferred_element_type=jnp.float32).astype(
        jnp.bfloat16
    )
    hidden = jnp.dot(own_half, mlp_in[:D], preferred_element_type=jnp.float32)
    hidden = (
        hidden + jnp.dot(projected, mlp_in[D:], preferred_element_type=jnp.float32) + mlp_in_bias
    )
    mean_value = jnp.mean(hidden, axis=1, keepdims=True)
    centered = hidden - mean_value
    variance = jnp.mean(centered * centered, axis=1, keepdims=True)
    normed = centered * lax.rsqrt(variance + 1e-05) * norm_gain + norm_bias
    activated = jax.nn.gelu(normed, approximate=False).astype(jnp.bfloat16)
    output_rows = jnp.dot(activated, mlp_out, preferred_element_type=jnp.float32) + mlp_out_bias
    output_rows = output_rows + own_half.astype(jnp.float32)
    return output_rows.astype(jnp.bfloat16)[None]


def solution(mesh):
    placed = (
        P(("groups", "img", "pair"), None, None),
        P("groups", None),
        P(None, "sub"),
        P(None, "sub"),
        P(),
        P(),
        P(),
        P(),
        P(),
        P(),
        P(),
    )
    return jax.shard_map(
        on_device,
        mesh=mesh,
        in_specs=placed,
        out_specs=P(("groups", "img", "pair"), "sub", None),
        check_vma=False,
    )
```

profile of v0, /device:TPU:17, one launch (start us, length us, event | category | flops | bytes accessed | tf_op | source)
XLA Modules:
  0.0 95.1 jit_solution(5887512537064446653)
XLA Ops:
  0.0 1.4 %convolution_convert_fusion.2 = bf16[1024,128]{0,1:T(8,128)(2,1)S(1)} fusion(bf16[256,128]{1,0:T(8,128)(2,1)} %param.13, bf16[1,1024,256]{2,1,0:T(8,128)(2,1)} %param.11), kind=kOutput, calls=%fused_computation.68 | convolution fusion | flops 67239936 | bytes 851968 | tf_op jit(solution)/shard_map/dot_general | solution.py:69
  1.4 1.4 %convolution_convert_fusion.1 = bf16[1024,128]{0,1:T(8,128)(2,1)S(1)} fusion(bf16[256,128]{1,0:T(8,128)(2,1)} %param.14, bf16[1,1024,256]{2,1,0:T(8,128)(2,1)} %param.11), kind=kOutput, calls=%fused_computation.67 | convolution fusion | flops 67239936 | bytes 851968 | tf_op jit(solution)/shard_map/dot_general | solution.py:70
  2.8 3.1 %collective-permute-start.5 = (bf16[1024,256]{0,1:T(8,128)(2,1)S(1)}, bf16[1024,256]{0,1:T(8,128)(2,1)}, u32[]{:S(2)}, u32[]{:S(2)}) collective-permute-start(bf16[1024,256]{0,1:T(8,128)(2,1)S(1)} %pad_maximum_fusion), channel_id=1, source_target_pairs={{0,2},{2,4},{4,6},{6,8},{8,10},{10,12},{12,14},{1,3},{3,5},{5,7},{... | collective-permute-start | bytes 1572872 | tf_op jit(solution)/shard_map/ppermute | solution.py:15
  5.9 3.2 %collective-permute-start.4 = (bf16[1024,256]{0,1:T(8,128)(2,1)S(1)}, bf16[1024,256]{0,1:T(8,128)(2,1)}, u32[]{:S(2)}, u32[]{:S(2)}) collective-permute-start(bf16[1024,256]{0,1:T(8,128)(2,1)S(1)} %pad_maximum_fusion), channel_id=1, source_target_pairs={{0,4},{2,6},{4,8},{6,10},{8,12},{10,14},{1,5},{3,7},{5,9},{7,11},{... | collective-permute-start | bytes 1572872 | tf_op jit(solution)/shard_map/ppermute | solution.py:15
  9.1 1.9 %collective-permute-start.3 = (bf16[1024,256]{0,1:T(8,128)(2,1)S(1)}, bf16[1024,256]{0,1:T(8,128)(2,1)}, u32[]{:S(2)}, u32[]{:S(2)}) collective-permute-start(bf16[1024,256]{0,1:T(8,128)(2,1)S(1)} %pad_maximum_fusion), channel_id=1, source_target_pairs={{0,6},{2,8},{4,10},{6,12},{8,14},{1,7},{3,9},{5,11},{7,13},{9,15},... | collective-permute-start | bytes 1572872 | tf_op jit(solution)/shard_map/ppermute | solution.py:15
  11.1 5.9 %collective-permute-start.2 = (bf16[1024,256]{0,1:T(8,128)(2,1)S(1)}, bf16[1024,256]{0,1:T(8,128)(2,1)S(1)}, u32[]{:S(2)}, u32[]{:S(2)}) collective-permute-start(bf16[1024,256]{0,1:T(8,128)(2,1)S(1)} %pad_maximum_fusion), channel_id=1, source_target_pairs={{6,0},{8,2},{10,4},{12,6},{14,8},{7,1},{9,3},{11,5},{13,7},{15,9},... | collective-permute-start | bytes 1572872 | tf_op jit(solution)/shard_map/ppermute | solution.py:15
  17.0 1.9 %collective-permute-start.1 = (bf16[1024,256]{0,1:T(8,128)(2,1)S(1)}, bf16[1024,256]{0,1:T(8,128)(2,1)S(1)}, u32[]{:S(2)}, u32[]{:S(2)}) collective-permute-start(bf16[1024,256]{0,1:T(8,128)(2,1)S(1)} %pad_maximum_fusion), channel_id=1, source_target_pairs={{4,0},{6,2},{8,4},{10,6},{12,8},{14,10},{5,1},{7,3},{9,5},{11,7},{... | collective-permute-start | bytes 1572872 | tf_op jit(solution)/shard_map/ppermute | solution.py:15
  19.0 1.6 %constant_dynamic-slice_fusion.1 = (s32[1,1]{0,1:T(1,128)}, s32[1,1]{0,1:T(1,128)}, s32[1,1]{0,1:T(1,128)}, s32[1,1]{0,1:T(1,128)}, s32[1,1]{0,1:T(1,128)}, /*index=5*/s32[1,1]{0,1:T(1,128)}) fusion(s32[8,3]{0,1:T(4,128)} %param.12, s32[]{:T(128)S(6)} %min.15, s32[]{:T(128)S(6)} %min.16, s32[]{:T(128)S(6)} %min.18, s32[]{:T(128)S(6)} %min.17), kind=kLoop, calls=%fused_computation.208 | loop fusion | bytes 64 | tf_op jit(solution)/shard_map/dynamic_slice | solution.py:21
  24.3 1.4 %fusion.87 = f32[512,512]{0,1:T(8,128)S(1)} fusion(bf16[512,512]{1,0:T(8,128)(2,1)} %param.16, bf16[1,1024,256]{2,1,0:T(8,128)(2,1)} %param.11, s32[]{:T(128)S(6)} %select_n.28), kind=kOutput, calls=%fused_computation.140 | convolution fusion | flops 134217728 | bytes 1572868 | tf_op jit(solution)/shard_map/dot_general | solution.py:94
  25.7 2.2 %collective-permute-start = (bf16[1024,256]{0,1:T(8,128)(2,1)S(1)}, bf16[1024,256]{0,1:T(8,128)(2,1)S(1)}, u32[]{:S(2)}, u32[]{:S(2)}) collective-permute-start(bf16[1024,256]{0,1:T(8,128)(2,1)S(1)} %pad_maximum_fusion), channel_id=1, source_target_pairs={{2,0},{4,2},{6,4},{8,6},{10,8},{12,10},{14,12},{3,1},{5,3},{7,5},{... | collective-permute-start | bytes 1572872 | tf_op jit(solution)/shard_map/ppermute | solution.py:15
  27.8 1.7 %multiply_reduce_fusion.1 = (f32[1024]{0:T(1024)S(1)}, f32[1024,1024]{0,1:T(8,128)S(1)}) fusion(bf16[1024,256]{0,1:T(8,128)(2,1)} %collective-permute-done.5, bf16[1024,128]{0,1:T(8,128)(2,1)S(1)} %convolution_convert_fusion.2), kind=kOutput, calls=%fused_computation.25 | convolution fusion | flops 136313856 | bytes 4460544 | tf_op jit(solution)/shard_map/qd,kd->qk/dot_general | solution.py:40
  29.5 1.7 %multiply_reduce_fusion = (f32[1024]{0:T(1024)S(1)}, f32[1024,1024]{0,1:T(8,128)S(1)}) fusion(bf16[1024,256]{0,1:T(8,128)(2,1)} %collective-permute-done.5, bf16[1024,128]{0,1:T(8,128)(2,1)S(1)} %convolution_convert_fusion.2), kind=kOutput, calls=%fused_computation.24 | convolution fusion | flops 136313856 | bytes 4460544 | tf_op jit(solution)/shard_map/qd,kd->qk/dot_general | solution.py:40
  32.7 1.7 %multiply_reduce_fusion.3 = (f32[1024]{0:T(1024)S(1)}, f32[1024,1024]{0,1:T(8,128)S(1)}) fusion(bf16[1024,256]{0,1:T(8,128)(2,1)} %collective-permute-done.4, bf16[1024,128]{0,1:T(8,128)(2,1)S(1)} %convolution_convert_fusion.2), kind=kOutput, calls=%fused_computation.27 | convolution fusion | flops 136313856 | bytes 4460544 | tf_op jit(solution)/shard_map/qd,kd->qk/dot_general | solution.py:40
  34.3 1.7 %multiply_reduce_fusion.2 = (f32[1024]{0:T(1024)S(1)}, f32[1024,1024]{0,1:T(8,128)S(1)}) fusion(bf16[1024,256]{0,1:T(8,128)(2,1)} %collective-permute-done.4, bf16[1024,128]{0,1:T(8,128)(2,1)S(1)} %convolution_convert_fusion.2), kind=kOutput, calls=%fused_computation.26 | convolution fusion | flops 136313856 | bytes 4460544 | tf_op jit(solution)/shard_map/qd,kd->qk/dot_general | solution.py:40
  37.5 3.5 %collective-permute-done.3 = bf16[1024,256]{0,1:T(8,128)(2,1)} collective-permute-done((bf16[1024,256]{0,1:T(8,128)(2,1)S(1)}, bf16[1024,256]{0,1:T(8,128)(2,1)}, u32[]{:S(2)}, u32[]{:S(2)}) %collective-permute-start.3) | collective-permute-done | bytes 524320 | tf_op jit(solution)/shard_map/ppermute | solution.py:15
  41.0 1.7 %multiply_reduce_fusion.5 = (f32[1024]{0:T(1024)S(1)}, f32[1024,1024]{0,1:T(8,128)S(1)}) fusion(bf16[1024,256]{0,1:T(8,128)(2,1)} %collective-permute-done.3, bf16[1024,128]{0,1:T(8,128)(2,1)S(1)} %convolution_convert_fusion.2), kind=kOutput, calls=%fused_computation.29 | convolution fusion | flops 136313856 | bytes 4460544 | tf_op jit(solution)/shard_map/qd,kd->qk/dot_general | solution.py:40
  43.4 1.7 %multiply_reduce_fusion.4 = (f32[1024]{0:T(1024)S(1)}, f32[1024,1024]{0,1:T(8,128)S(1)}) fusion(bf16[1024,256]{0,1:T(8,128)(2,1)} %collective-permute-done.3, bf16[1024,128]{0,1:T(8,128)(2,1)S(1)} %convolution_convert_fusion.2), kind=kOutput, calls=%fused_computation.28 | convolution fusion | flops 136313856 | bytes 4460544 | tf_op jit(solution)/shard_map/qd,kd->qk/dot_general | solution.py:40
  45.1 1.9 %fusion.29 = bf16[1024,64]{0,1:T(8,128)(2,1)S(1)} fusion(f32[1024,1024]{0,1:T(8,128)S(1)} %get-tuple-element.34, f32[1024]{0:T(1024)S(1)} %fusion.10, f32[1024]{0:T(1024)S(1)} %get-tuple-element.33, bf16[1024,256]{0,1:T(8,128)(2,1)} %collective-permute-done.5), kind=kOutput, calls=%fused_computation.71 | convolution fusion | flops 138477568 | bytes 4464640 | tf_op jit(solution)/shard_map/dot_general | solution.py:45
  46.9 1.9 %fusion.28 = bf16[1024,64]{0,1:T(8,128)(2,1)S(1)} fusion(f32[1024,1024]{0,1:T(8,128)S(1)} %get-tuple-element.32, f32[1024]{0:T(1024)S(1)} %fusion.11, f32[1024]{0:T(1024)S(1)} %get-tuple-element.31, bf16[1024,256]{0,1:T(8,128)(2,1)} %collective-permute-done.5), kind=kOutput, calls=%fused_computation.70 | convolution fusion | flops 138477568 | bytes 4464640 | tf_op jit(solution)/shard_map/dot_general | solution.py:45
  51.0 1.0 %multiply_reduce_fusion.6 = (f32[1024]{0:T(1024)S(1)}, f32[1024,1024]{0,1:T(8,128)S(1)}) fusion(bf16[1024,256]{0,1:T(8,128)(2,1)S(1)} %collective-permute-done.2, bf16[1024,128]{0,1:T(8,128)(2,1)S(1)} %convolution_convert_fusion.2), kind=kOutput, calls=%fused_computation.30 | convolution fusion | flops 136313856 | bytes 4460544 | tf_op jit(solution)/shard_map/qd,kd->qk/dot_general | solution.py:40
  52.0 1.9 %fusion.31 = bf16[1024,64]{0,1:T(8,128)(2,1)S(1)} fusion(f32[1024,1024]{0,1:T(8,128)S(1)} %get-tuple-element.30, f32[1024]{0:T(1024)S(1)} %fusion.8, f32[1024]{0:T(1024)S(1)} %get-tuple-element.29, bf16[1024,256]{0,1:T(8,128)(2,1)} %collective-permute-done.4), kind=kOutput, calls=%fused_computation.73 | convolution fusion | flops 138477568 | bytes 4464640 | tf_op jit(solution)/shard_map/dot_general | solution.py:45
  53.9 1.9 %fusion.30 = bf16[1024,64]{0,1:T(8,128)(2,1)S(1)} fusion(f32[1024,1024]{0,1:T(8,128)S(1)} %get-tuple-element.28, f32[1024]{0:T(1024)S(1)} %fusion.9, f32[1024]{0:T(1024)S(1)} %get-tuple-element.27, bf16[1024,256]{0,1:T(8,128)(2,1)} %collective-permute-done.4), kind=kOutput, calls=%fused_computation.72 | convolution fusion | flops 138477568 | bytes 4464640 | tf_op jit(solution)/shard_map/dot_general | solution.py:45
  59.5 1.9 %fusion.33 = bf16[1024,64]{0,1:T(8,128)(2,1)S(1)} fusion(f32[1024,1024]{0,1:T(8,128)S(1)} %get-tuple-element.26, f32[1024]{0:T(1024)S(1)} %fusion.6, f32[1024]{0:T(1024)S(1)} %get-tuple-element.25, bf16[1024,256]{0,1:T(8,128)(2,1)} %collective-permute-done.3), kind=kOutput, calls=%fused_computation.75 | convolution fusion | flops 138477568 | bytes 4464640 | tf_op jit(solution)/shard_map/dot_general | solution.py:45
  61.4 1.9 %fusion.32 = bf16[1024,64]{0,1:T(8,128)(2,1)S(1)} fusion(f32[1024,1024]{0,1:T(8,128)S(1)} %get-tuple-element.24, f32[1024]{0:T(1024)S(1)} %fusion.7, f32[1024]{0:T(1024)S(1)} %get-tuple-element.23, bf16[1024,256]{0,1:T(8,128)(2,1)} %collective-permute-done.3), kind=kOutput, calls=%fused_computation.74 | convolution fusion | flops 138477568 | bytes 4464640 | tf_op jit(solution)/shard_map/dot_general | solution.py:45
  63.2 1.0 %fusion.35 = bf16[1024,64]{0,1:T(8,128)(2,1)S(1)} fusion(f32[1024,1024]{0,1:T(8,128)S(1)} %get-tuple-element.22, f32[1024]{0:T(1024)S(1)} %fusion.4, f32[1024]{0:T(1024)S(1)} %get-tuple-element.21, bf16[1024,256]{0,1:T(8,128)(2,1)S(1)} %collective-permute-done.2), kind=kOutput, calls=%fused_computation.77 | convolution fusion | flops 138477568 | bytes 4464640 | tf_op jit(solution)/shard_map/dot_general | solution.py:45
  64.2 1.0 %fusion.34 = bf16[1024,64]{0,1:T(8,128)(2,1)S(1)} fusion(f32[1024,1024]{0,1:T(8,128)S(1)} %get-tuple-element.20, f32[1024]{0:T(1024)S(1)} %fusion.5, f32[1024]{0:T(1024)S(1)} %get-tuple-element.19, bf16[1024,256]{0,1:T(8,128)(2,1)S(1)} %collective-permute-done.2), kind=kOutput, calls=%fused_computation.76 | convolution fusion | flops 138477568 | bytes 4464640 | tf_op jit(solution)/shard_map/dot_general | solution.py:45
  65.2 1.0 %fusion.37 = bf16[1024,64]{0,1:T(8,128)(2,1)S(1)} fusion(f32[1024,1024]{0,1:T(8,128)S(1)} %get-tuple-element.18, f32[1024]{0:T(1024)S(1)} %fusion.2, f32[1024]{0:T(1024)S(1)} %get-tuple-element.17, bf16[1024,256]{0,1:T(8,128)(2,1)S(1)} %collective-permute-done.1), kind=kOutput, calls=%fused_computation.79 | convolution fusion | flops 138477568 | bytes 4464640 | tf_op jit(solution)/shard_map/dot_general | solution.py:45
  66.1 1.0 %fusion.36 = bf16[1024,64]{0,1:T(8,128)(2,1)S(1)} fusion(f32[1024,1024]{0,1:T(8,128)S(1)} %get-tuple-element.16, f32[1024]{0:T(1024)S(1)} %fusion.3, f32[1024]{0:T(1024)S(1)} %get-tuple-element.15, bf16[1024,256]{0,1:T(8,128)(2,1)S(1)} %collective-permute-done.1), kind=kOutput, calls=%fused_computation.78 | convolution fusion | flops 138477568 | bytes 4464640 | tf_op jit(solution)/shard_map/dot_general | solution.py:45
  71.4 1.0 %fusion.38 = bf16[1024,64]{0,1:T(8,128)(2,1)S(1)} fusion(f32[1024,1024]{0,1:T(8,128)S(1)} %get-tuple-element.12, f32[1024]{0:T(1024)S(1)} %fusion.1, f32[1024]{0:T(1024)S(1)} %get-tuple-element.11, bf16[1024,256]{0,1:T(8,128)(2,1)S(1)} %collective-permute-done), kind=kOutput, calls=%fused_computation.80 | convolution fusion | flops 138477568 | bytes 4464640 | tf_op jit(solution)/shard_map/dot_general | solution.py:45
  72.7 17.1 %all_to_all.16 = bf16[2,512,128]{1,2,0:T(8,128)(2,1)S(1)} all-to-all(bf16[2,512,128]{1,2,0:T(8,128)(2,1)S(1)} %add_convert_fusion), channel_id=1, replica_groups=mesh['groups'=2,'img'=4,'pair'=2,'sub'=2] {'sub'}, dimensions={0} | all-to-all | bytes 524288 | tf_op jit(solution)/shard_map/all_to_all | solution.py:90
  89.8 1.5 %fusion.183 = (f32[512]{0:T(512)S(1)}, f32[512,512]{0,1:T(8,128)S(1)}) fusion(f32[512]{0:T(512)S(1)} %copy-done.3, f32[512,512]{0,1:T(8,128)S(1)} %fusion.87, bf16[512,512]{1,0:T(8,128)(2,1)} %param.16, bf16[512,256]{0,1:T(8,128)(2,1)S(1)} %bitcast.61, bf16[256,256]{1,0:T(8,128)(2,1)S(1)} %copy-done.2), kind=kOutput, calls=%fused_computation.256 | convolution fusion | flops 202243584 | bytes 2756608 | tf_op jit(solution)/shard_map/dot_general | solution.py:96
  91.6 3.5 %fusion.27 = bf16[1,512,256]{2,1,0:T(8,128)(2,1)} fusion(bf16[512,256]{1,0:T(8,128)(2,1)S(1)} %copy-done, f32[512,512]{0,1:T(8,128)S(1)} %get-tuple-element.36, f32[512]{0:T(512)S(1)} %copy-done.4, f32[512]{0:T(512)S(1)} %copy-done.5, f32[512]{0:T(512)S(1)} %add_rsqrt_fusion, f32[512]{0:T(512)S(1)} %broadcast_multiply_fusion, f32[256]{0:T(256)S(1)} %copy-done.6, ...), kind=kOutput, calls=%fused_computation.69 | convolution fusion | flops 152829952 | bytes 1844228 | tf_op jit(solution)/shard_map/dot_general | solution.py:103
  (48 shorter events, 14.5 us)
Async XLA Ops:
  0.0 91.6 %copy-start = (bf16[512,256]{1,0:T(8,128)(2,1)S(1)}, bf16[512,256]{1,0:T(8,128)(2,1)}, u32[]{:S(2)}) copy-start(bf16[512,256]{1,0:T(8,128)(2,1)} %param.20) | copy-start | bytes 786436
  2.8 22.9 %collective-permute-start.5 = (bf16[1024,256]{0,1:T(8,128)(2,1)S(1)}, bf16[1024,256]{0,1:T(8,128)(2,1)}, u32[]{:S(2)}, u32[]{:S(2)}) collective-permute-start(bf16[1024,256]{0,1:T(8,128)(2,1)S(1)} %pad_maximum_fusion), channel_id=1, source_target_pairs={{0,2},{2,4},{4,6},{6,8},{8,10},{10,12},{12,14},{1,3},{3,5},{5,7},{... | collective-permute-start | bytes 1572872 | tf_op jit(solution)/shard_map/ppermute | solution.py:15
  5.9 26.7 %collective-permute-start.4 = (bf16[1024,256]{0,1:T(8,128)(2,1)S(1)}, bf16[1024,256]{0,1:T(8,128)(2,1)}, u32[]{:S(2)}, u32[]{:S(2)}) collective-permute-start(bf16[1024,256]{0,1:T(8,128)(2,1)S(1)} %pad_maximum_fusion), channel_id=1, source_target_pairs={{0,4},{2,6},{4,8},{6,10},{8,12},{10,14},{1,5},{3,7},{5,9},{7,11},{... | collective-permute-start | bytes 1572872 | tf_op jit(solution)/shard_map/ppermute | solution.py:15
  9.1 31.8 %collective-permute-start.3 = (bf16[1024,256]{0,1:T(8,128)(2,1)S(1)}, bf16[1024,256]{0,1:T(8,128)(2,1)}, u32[]{:S(2)}, u32[]{:S(2)}) collective-permute-start(bf16[1024,256]{0,1:T(8,128)(2,1)S(1)} %pad_maximum_fusion), channel_id=1, source_target_pairs={{0,6},{2,8},{4,10},{6,12},{8,14},{1,7},{3,9},{5,11},{7,13},{9,15},... | collective-permute-start | bytes 1572872 | tf_op jit(solution)/shard_map/ppermute | solution.py:15
  11.1 38.5 %collective-permute-start.2 = (bf16[1024,256]{0,1:T(8,128)(2,1)S(1)}, bf16[1024,256]{0,1:T(8,128)(2,1)S(1)}, u32[]{:S(2)}, u32[]{:S(2)}) collective-permute-start(bf16[1024,256]{0,1:T(8,128)(2,1)S(1)} %pad_maximum_fusion), channel_id=1, source_target_pairs={{6,0},{8,2},{10,4},{12,6},{14,8},{7,1},{9,3},{11,5},{13,7},{15,9},... | collective-permute-start | bytes 1572872 | tf_op jit(solution)/shard_map/ppermute | solution.py:15
  17.0 39.5 %collective-permute-start.1 = (bf16[1024,256]{0,1:T(8,128)(2,1)S(1)}, bf16[1024,256]{0,1:T(8,128)(2,1)S(1)}, u32[]{:S(2)}, u32[]{:S(2)}) collective-permute-start(bf16[1024,256]{0,1:T(8,128)(2,1)S(1)} %pad_maximum_fusion), channel_id=1, source_target_pairs={{4,0},{6,2},{8,4},{10,6},{12,8},{14,10},{5,1},{7,3},{9,5},{11,7},{... | collective-permute-start | bytes 1572872 | tf_op jit(solution)/shard_map/ppermute | solution.py:15
  25.7 41.5 %collective-permute-start = (bf16[1024,256]{0,1:T(8,128)(2,1)S(1)}, bf16[1024,256]{0,1:T(8,128)(2,1)S(1)}, u32[]{:S(2)}, u32[]{:S(2)}) collective-permute-start(bf16[1024,256]{0,1:T(8,128)(2,1)S(1)} %pad_maximum_fusion), channel_id=1, source_target_pairs={{2,0},{4,2},{6,4},{8,6},{10,8},{12,10},{14,12},{3,1},{5,3},{7,5},{... | collective-permute-start | bytes 1572872 | tf_op jit(solution)/shard_map/ppermute | solution.py:15
  71.4 18.5 %copy-start.2 = (bf16[256,256]{1,0:T(8,128)(2,1)S(1)}, bf16[256,256]{1,0:T(8,128)(2,1)}, u32[]{:S(2)}) copy-start(bf16[256,256]{1,0:T(8,128)(2,1)} %param.15) | copy-start | bytes 393220
  71.4 18.5 %copy-start.3 = (f32[512]{0:T(512)S(1)}, f32[512]{0:T(512)}, u32[]{:S(2)}) copy-start(f32[512]{0:T(512)} %param.17) | copy-start | bytes 6148
  72.3 19.2 %copy-start.1 = (bf16[1,1024,256]{2,1,0:T(8,128)(2,1)S(1)}, bf16[1,1024,256]{2,1,0:T(8,128)(2,1)}, u32[]{:S(2)}) copy-start(bf16[1,1024,256]{2,1,0:T(8,128)(2,1)} %param.11) | copy-start | bytes 1572868
  72.3 19.2 %copy-start.4 = (f32[512]{0:T(512)S(1)}, f32[512]{0:T(512)}, u32[]{:S(2)}) copy-start(f32[512]{0:T(512)} %param.19) | copy-start | bytes 6148
  72.4 19.2 %copy-start.5 = (f32[512]{0:T(512)S(1)}, f32[512]{0:T(512)}, u32[]{:S(2)}) copy-start(f32[512]{0:T(512)} %param.18) | copy-start | bytes 6148
  72.4 19.2 %copy-start.6 = (f32[256]{0:T(256)S(1)}, f32[256]{0:T(256)}, u32[]{:S(2)}) copy-start(f32[256]{0:T(256)} %param.21) | copy-start | bytes 3076
where the time goes:
time: 95.8 us; the launch traced here: 95.1 us
  matrix products  40.8 us (43%)
  starting transfers between devices  18.3 us (19%)
  blocking collectives  17.1 us (18%)
  other arithmetic  9.53 us (10%)
  between operations  4.11 us (4%)
  waiting for transfers between devices  3.54 us (4%)
  local copies, waits for them, and re-layouts  1.74 us (2%)
    ppermute x6, starting transfers between devices, passed_along(): return lax.ppermute(value, axis, pairs)  18.3 us
    all_to_all x1, blocking collectives, on_device(): lax.all_to_all(summed_b, 'sub', split_axis=0, concat_axis=1, tiled=True)  17.1 us
    dot_general x12, matrix products, tile_messages(): jnp.dot(row_weights, partner_values[:, lo_col:lo_col + head_width], prefe...  16.9 us
    dot_general x12, matrix products, tile_messages(): jnp.einsum('qd,kd->qk', query_part, key_part, preferred_element_type=jnp....  14.8 us
    reduce_sum x12, other arithmetic, tile_messages(): row_weights = jax.nn.softmax(scores, axis=1).astype(jnp.bfloat16)  8.99 us
    ppermute x6, waiting for transfers between devices, passed_along(): return lax.ppermute(value, axis, pairs)  3.54 us
    dot_general x1, matrix products, on_device(): jnp.dot(activated, mlp_out, preferred_element_type=jnp.float32)  3.52 us
  transfers between devices with their start and end apart: 6, of which 1 were waited for; matrix products, arithmetic and copies ran while one was open for 41% of the time, Pallas kernels for 0%

commit v1 on v0

--- a/solution.py
+++ b/solution.py
@@ -87,7 +87,10 @@
         message, unused = tile_messages(key_rows, partner_keys, partner_values)
         summed = summed + linked * message.astype(jnp.float32)
     summed_b = summed.astype(jnp.bfloat16)
-    gathered = lax.all_to_all(summed_b, "sub", split_axis=0, concat_axis=1, tiled=True)
+    gathered = jnp.concatenate(
+        lax.all_to_all(jnp.stack(jnp.split(summed_b, lax.axis_size("sub"), axis=0)), "sub", 0, 0),
+        axis=1,
+    )
     projected = jnp.dot(gathered, out_weight, preferred_element_type=jnp.float32).astype(
         jnp.bfloat16
     )

time: 95.8 us -> 110 us (1.15)
  waiting for transfers between devices: 3.54 us -> 12.1 us
  matrix products: 40.8 us -> 48.9 us
  blocking collectives: 17.1 us -> 9.18 us
  other arithmetic: 9.53 us -> 13.7 us
  local copies, waits for them, and re-layouts: 1.74 us -> 3.12 us
    ppermute x6, waiting for transfers between devices: 3.54 us -> 12.1 us  [passed_along(): return lax.ppermute(value, axis, pairs)]
    all_to_all x1, blocking collectives: 17.1 us -> 9.18 us  [on_device(): lax.all_to_all(jnp.stack(jnp.split(summed_b, lax.axis_size('sub'), axis=0...]
    dot_general x12, matrix products: 14.8 us -> 20.5 us  [tile_messages(): jnp.einsum('qd,kd->qk', query_part, key_part, preferred_element_type=jnp....]
    reduce_sum x12, other arithmetic: 8.99 us -> 13.1 us  [tile_messages(): row_weights = jax.nn.softmax(scores, axis=1).astype(jnp.bfloat16)]
    dot_general x12, matrix products: 16.9 us -> 19.1 us  [tile_messages(): jnp.dot(row_weights, partner_values[:, lo_col:lo_col + head_width], prefe...]
    unnamed x14 -> x20, local copies, waits for them, and re-layouts: 0.04 us -> 1.52 us
  transfers between devices with their start and end apart: 6 -> 6, of which waited for: 1 -> 3; matrix products, arithmetic and copies ran while one was open for 41% -> 21% of each run, Pallas kernels for 0% -> 0%
where the time goes in v1:
time: 110 us; the launch traced here: 109 us
  matrix products  48.9 us (44%)
  starting transfers between devices  18.3 us (17%)
  other arithmetic  13.7 us (12%)
  waiting for transfers between devices  12.1 us (11%)
  blocking collectives  9.18 us (8%)
  between operations  4.14 us (4%)
  local copies, waits for them, and re-layouts  3.12 us (3%)
    dot_general x12, matrix products, tile_messages(): jnp.einsum('qd,kd->qk', query_part, key_part, preferred_element_type=jnp....  20.5 us
    dot_general x12, matrix products, tile_messages(): jnp.dot(row_weights, partner_values[:, lo_col:lo_col + head_width], prefe...  19.1 us
    ppermute x6, starting transfers between devices, passed_along(): return lax.ppermute(value, axis, pairs)  18.3 us
    reduce_sum x12, other arithmetic, tile_messages(): row_weights = jax.nn.softmax(scores, axis=1).astype(jnp.bfloat16)  13.1 us
    ppermute x6, waiting for transfers between devices, passed_along(): return lax.ppermute(value, axis, pairs)  12.1 us
    all_to_all x1, blocking collectives, on_device(): lax.all_to_all(jnp.stack(jnp.split(summed_b, lax.axis_size('sub'), axis=0...  9.18 us
    dot_general x1, matrix products, on_device(): jnp.dot(activated, mlp_out, preferred_element_type=jnp.float32)  3.52 us
  transfers between devices with their start and end apart: 6, of which 3 were waited for; matrix products, arithmetic and copies ran while one was open for 21% of the time, Pallas kernels for 0%

profile of v1, /device:TPU:17, one launch (start us, length us, event | category | flops | bytes accessed | tf_op | source)
XLA Modules:
  0.0 109.5 jit_solution(97318247557640523)
XLA Ops:
  0.0 1.4 %convolution_convert_fusion.2 = bf16[1024,128]{0,1:T(8,128)(2,1)S(1)} fusion(bf16[256,128]{1,0:T(8,128)(2,1)} %param.13, bf16[1,1024,256]{2,1,0:T(8,128)(2,1)} %param.11), kind=kOutput, calls=%fused_computation.68 | convolution fusion | flops 67239936 | bytes 851968 | tf_op jit(solution)/shard_map/dot_general | solution.py:69
  2.8 3.1 %collective-permute-start.5 = (bf16[1024,256]{0,1:T(8,128)(2,1)S(1)}, bf16[1024,256]{0,1:T(8,128)(2,1)}, u32[]{:S(2)}, u32[]{:S(2)}) collective-permute-start(bf16[1024,256]{0,1:T(8,128)(2,1)S(1)} %pad_maximum_fusion), channel_id=1, source_target_pairs={{0,2},{2,4},{4,6},{6,8},{8,10},{10,12},{12,14},{1,3},{3,5},{5,7},{... | collective-permute-start | bytes 1572872 | tf_op jit(solution)/shard_map/ppermute | solution.py:15
  5.9 3.2 %collective-permute-start.4 = (bf16[1024,256]{0,1:T(8,128)(2,1)S(1)}, bf16[1024,256]{0,1:T(8,128)(2,1)}, u32[]{:S(2)}, u32[]{:S(2)}) collective-permute-start(bf16[1024,256]{0,1:T(8,128)(2,1)S(1)} %pad_maximum_fusion), channel_id=1, source_target_pairs={{0,4},{2,6},{4,8},{6,10},{8,12},{10,14},{1,5},{3,7},{5,9},{7,11},{... | collective-permute-start | bytes 1572872 | tf_op jit(solution)/shard_map/ppermute | solution.py:15
  9.1 1.9 %collective-permute-start.3 = (bf16[1024,256]{0,1:T(8,128)(2,1)S(1)}, bf16[1024,256]{0,1:T(8,128)(2,1)}, u32[]{:S(2)}, u32[]{:S(2)}) collective-permute-start(bf16[1024,256]{0,1:T(8,128)(2,1)S(1)} %pad_maximum_fusion), channel_id=1, source_target_pairs={{0,6},{2,8},{4,10},{6,12},{8,14},{1,7},{3,9},{5,11},{7,13},{9,15},... | collective-permute-start | bytes 1572872 | tf_op jit(solution)/shard_map/ppermute | solution.py:15
  11.1 6.0 %collective-permute-start.2 = (bf16[1024,256]{0,1:T(8,128)(2,1)S(1)}, bf16[1024,256]{0,1:T(8,128)(2,1)S(1)}, u32[]{:S(2)}, u32[]{:S(2)}) collective-permute-start(bf16[1024,256]{0,1:T(8,128)(2,1)S(1)} %pad_maximum_fusion), channel_id=1, source_target_pairs={{6,0},{8,2},{10,4},{12,6},{14,8},{7,1},{9,3},{11,5},{13,7},{15,9},... | collective-permute-start | bytes 1572872 | tf_op jit(solution)/shard_map/ppermute | solution.py:15
  17.1 1.9 %collective-permute-start.1 = (bf16[1024,256]{0,1:T(8,128)(2,1)S(1)}, bf16[1024,256]{0,1:T(8,128)(2,1)S(1)}, u32[]{:S(2)}, u32[]{:S(2)}) collective-permute-start(bf16[1024,256]{0,1:T(8,128)(2,1)S(1)} %pad_maximum_fusion), channel_id=1, source_target_pairs={{4,0},{6,2},{8,4},{10,6},{12,8},{14,10},{5,1},{7,3},{9,5},{11,7},{... | collective-permute-start | bytes 1572872 | tf_op jit(solution)/shard_map/ppermute | solution.py:15
  19.0 1.6 %constant_dynamic-slice_fusion.1 = (s32[1,1]{0,1:T(1,128)}, s32[1,1]{0,1:T(1,128)}, s32[1,1]{0,1:T(1,128)}, s32[1,1]{0,1:T(1,128)}, s32[1,1]{0,1:T(1,128)}, /*index=5*/s32[1,1]{0,1:T(1,128)}) fusion(s32[8,3]{0,1:T(4,128)} %param.12, s32[]{:T(128)S(6)} %min.15, s32[]{:T(128)S(6)} %min.16, s32[]{:T(128)S(6)} %min.18, s32[]{:T(128)S(6)} %min.17), kind=kLoop, calls=%fused_computation.199 | loop fusion | bytes 64 | tf_op jit(solution)/shard_map/dynamic_slice | solution.py:21
  24.4 1.4 %fusion.87 = f32[512,512]{0,1:T(8,128)S(1)} fusion(bf16[512,512]{1,0:T(8,128)(2,1)} %param.16, bf16[1,1024,256]{2,1,0:T(8,128)(2,1)} %param.11, s32[]{:T(128)S(6)} %select_n.28), kind=kOutput, calls=%fused_computation.141 | convolution fusion | flops 134217728 | bytes 1572868 | tf_op jit(solution)/shard_map/dot_general | solution.py:97
  25.8 2.2 %collective-permute-start = (bf16[1024,256]{0,1:T(8,128)(2,1)S(1)}, bf16[1024,256]{0,1:T(8,128)(2,1)}, u32[]{:S(2)}, u32[]{:S(2)}) collective-permute-start(bf16[1024,256]{0,1:T(8,128)(2,1)S(1)} %pad_maximum_fusion), channel_id=1, source_target_pairs={{2,0},{4,2},{6,4},{8,6},{10,8},{12,10},{14,12},{3,1},{5,3},{7,5},{... | collective-permute-start | bytes 1572872 | tf_op jit(solution)/shard_map/ppermute | solution.py:15
  28.0 1.7 %multiply_reduce_fusion = (f32[1024]{0:T(1024)S(1)}, f32[1024,1024]{0,1:T(8,128)S(1)}) fusion(bf16[1024,256]{0,1:T(8,128)(2,1)} %collective-permute-done.5, bf16[1024,128]{0,1:T(8,128)(2,1)S(1)} %convolution_convert_fusion.2), kind=kOutput, calls=%fused_computation.24 | convolution fusion | flops 136313856 | bytes 4460544 | tf_op jit(solution)/shard_map/qd,kd->qk/dot_general | solution.py:40
  29.6 1.7 %multiply_reduce_fusion.1 = (f32[1024]{0:T(1024)S(1)}, f32[1024,1024]{0,1:T(8,128)S(1)}) fusion(bf16[1024,256]{0,1:T(8,128)(2,1)} %collective-permute-done.5, bf16[1024,128]{0,1:T(8,128)(2,1)S(1)} %convolution_convert_fusion.2), kind=kOutput, calls=%fused_computation.25 | convolution fusion | flops 136313856 | bytes 4460544 | tf_op jit(solution)/shard_map/qd,kd->qk/dot_general | solution.py:40
  32.8 1.7 %multiply_reduce_fusion.2 = (f32[1024]{0:T(1024)S(1)}, f32[1024,1024]{0,1:T(8,128)S(1)}) fusion(bf16[1024,256]{0,1:T(8,128)(2,1)} %collective-permute-done.4, bf16[1024,128]{0,1:T(8,128)(2,1)S(1)} %convolution_convert_fusion.2), kind=kOutput, calls=%fused_computation.26 | convolution fusion | flops 136313856 | bytes 4460544 | tf_op jit(solution)/shard_map/qd,kd->qk/dot_general | solution.py:40
  34.5 1.7 %multiply_reduce_fusion.3 = (f32[1024]{0:T(1024)S(1)}, f32[1024,1024]{0,1:T(8,128)S(1)}) fusion(bf16[1024,256]{0,1:T(8,128)(2,1)} %collective-permute-done.4, bf16[1024,128]{0,1:T(8,128)(2,1)S(1)} %convolution_convert_fusion.2), kind=kOutput, calls=%fused_computation.27 | convolution fusion | flops 136313856 | bytes 4460544 | tf_op jit(solution)/shard_map/qd,kd->qk/dot_general | solution.py:40
  37.6 3.4 %collective-permute-done.3 = bf16[1024,256]{0,1:T(8,128)(2,1)} collective-permute-done((bf16[1024,256]{0,1:T(8,128)(2,1)S(1)}, bf16[1024,256]{0,1:T(8,128)(2,1)}, u32[]{:S(2)}, u32[]{:S(2)}) %collective-permute-start.3) | collective-permute-done | bytes 524320 | tf_op jit(solution)/shard_map/ppermute | solution.py:15
  41.0 1.7 %multiply_reduce_fusion.4 = (f32[1024]{0:T(1024)S(1)}, f32[1024,1024]{0,1:T(8,128)S(1)}) fusion(bf16[1024,256]{0,1:T(8,128)(2,1)} %collective-permute-done.3, bf16[1024,128]{0,1:T(8,128)(2,1)S(1)} %convolution_convert_fusion.2), kind=kOutput, calls=%fused_computation.28 | convolution fusion | flops 136313856 | bytes 4460544 | tf_op jit(solution)/shard_map/qd,kd->qk/dot_general | solution.py:40
  42.7 1.7 %multiply_reduce_fusion.5 = (f32[1024]{0:T(1024)S(1)}, f32[1024,1024]{0,1:T(8,128)S(1)}) fusion(bf16[1024,256]{0,1:T(8,128)(2,1)} %collective-permute-done.3, bf16[1024,128]{0,1:T(8,128)(2,1)S(1)} %convolution_convert_fusion.2), kind=kOutput, calls=%fused_computation.29 | convolution fusion | flops 136313856 | bytes 4460544 | tf_op jit(solution)/shard_map/qd,kd->qk/dot_general | solution.py:40
  52.7 8.0 %collective-permute-done = bf16[1024,256]{0,1:T(8,128)(2,1)} collective-permute-done((bf16[1024,256]{0,1:T(8,128)(2,1)S(1)}, bf16[1024,256]{0,1:T(8,128)(2,1)}, u32[]{:S(2)}, u32[]{:S(2)}) %collective-permute-start) | collective-permute-done | bytes 524320 | tf_op jit(solution)/shard_map/ppermute | solution.py:15
  60.7 3.6 %multiply_reduce_fusion.11 = (f32[1024]{0:T(1024)S(1)}, f32[1024,1024]{0,1:T(8,128)}) fusion(bf16[1024,256]{0,1:T(8,128)(2,1)} %collective-permute-done, bf16[1024,128]{0,1:T(8,128)(2,1)S(1)} %convolution_convert_fusion.2), kind=kOutput, calls=%fused_computation.35 | convolution fusion | flops 136313856 | bytes 4460544 | tf_op jit(solution)/shard_map/qd,kd->qk/dot_general | solution.py:40
  64.3 2.9 %fusion = f32[1024]{0:T(1024)S(1)} fusion(f32[1024,1024]{0,1:T(8,128)} %get-tuple-element.16, f32[1024]{0:T(1024)S(1)} %get-tuple-element.15), kind=kLoop, calls=%fused_computation.36 | loop fusion | flops 3144704 | bytes 4202496 | tf_op jit(solution)/shard_map/reduce_sum | solution.py:43
  67.2 3.6 %multiply_reduce_fusion.10 = (f32[1024]{0:T(1024)S(1)}, f32[1024,1024]{0,1:T(8,128)}) fusion(bf16[1024,256]{0,1:T(8,128)(2,1)} %collective-permute-done, bf16[1024,128]{0,1:T(8,128)(2,1)S(1)} %convolution_convert_fusion.2), kind=kOutput, calls=%fused_computation.34 | convolution fusion | flops 136313856 | bytes 4460544 | tf_op jit(solution)/shard_map/qd,kd->qk/dot_general | solution.py:40
  70.8 2.9 %fusion.1 = f32[1024]{0:T(1024)S(1)} fusion(f32[1024,1024]{0,1:T(8,128)} %get-tuple-element.14, f32[1024]{0:T(1024)S(1)} %get-tuple-element.13), kind=kLoop, calls=%fused_computation.37 | loop fusion | flops 3144704 | bytes 4202496 | tf_op jit(solution)/shard_map/reduce_sum | solution.py:43
  73.8 1.9 %fusion.28 = bf16[1024,64]{0,1:T(8,128)(2,1)S(1)} fusion(f32[1024,1024]{0,1:T(8,128)S(1)} %get-tuple-element.34, f32[1024]{0:T(1024)S(1)} %fusion.11, f32[1024]{0:T(1024)S(1)} %get-tuple-element.33, bf16[1024,256]{0,1:T(8,128)(2,1)} %collective-permute-done.5), kind=kOutput, calls=%fused_computation.70 | convolution fusion | flops 138477568 | bytes 4464640 | tf_op jit(solution)/shard_map/dot_general | solution.py:45
  75.6 1.9 %fusion.29 = bf16[1024,64]{0,1:T(8,128)(2,1)S(1)} fusion(f32[1024,1024]{0,1:T(8,128)S(1)} %get-tuple-element.36, f32[1024]{0:T(1024)S(1)} %fusion.10, f32[1024]{0:T(1024)S(1)} %get-tuple-element.35, bf16[1024,256]{0,1:T(8,128)(2,1)} %collective-permute-done.5), kind=kOutput, calls=%fused_computation.71 | convolution fusion | flops 138477568 | bytes 4464640 | tf_op jit(solution)/shard_map/dot_general | solution.py:45
  77.5 1.9 %fusion.30 = bf16[1024,64]{0,1:T(8,128)(2,1)S(1)} fusion(f32[1024,1024]{0,1:T(8,128)S(1)} %get-tuple-element.30, f32[1024]{0:T(1024)S(1)} %fusion.9, f32[1024]{0:T(1024)S(1)} %get-tuple-element.29, bf16[1024,256]{0,1:T(8,128)(2,1)} %collective-permute-done.4), kind=kOutput, calls=%fused_computation.72 | convolution fusion | flops 138477568 | bytes 4464640 | tf_op jit(solution)/shard_map/dot_general | solution.py:45
  79.3 1.9 %fusion.31 = bf16[1024,64]{0,1:T(8,128)(2,1)S(1)} fusion(f32[1024,1024]{0,1:T(8,128)S(1)} %get-tuple-element.32, f32[1024]{0:T(1024)S(1)} %fusion.8, f32[1024]{0:T(1024)S(1)} %get-tuple-element.31, bf16[1024,256]{0,1:T(8,128)(2,1)} %collective-permute-done.4), kind=kOutput, calls=%fused_computation.73 | convolution fusion | flops 138477568 | bytes 4464640 | tf_op jit(solution)/shard_map/dot_general | solution.py:45
  81.2 1.9 %fusion.32 = bf16[1024,64]{0,1:T(8,128)(2,1)S(1)} fusion(f32[1024,1024]{0,1:T(8,128)S(1)} %get-tuple-element.26, f32[1024]{0:T(1024)S(1)} %fusion.7, f32[1024]{0:T(1024)S(1)} %get-tuple-element.25, bf16[1024,256]{0,1:T(8,128)(2,1)} %collective-permute-done.3), kind=kOutput, calls=%fused_computation.74 | convolution fusion | flops 138477568 | bytes 4464640 | tf_op jit(solution)/shard_map/dot_general | solution.py:45
  83.1 1.9 %fusion.33 = bf16[1024,64]{0,1:T(8,128)(2,1)S(1)} fusion(f32[1024,1024]{0,1:T(8,128)S(1)} %get-tuple-element.28, f32[1024]{0:T(1024)S(1)} %fusion.6, f32[1024]{0:T(1024)S(1)} %get-tuple-element.27, bf16[1024,256]{0,1:T(8,128)(2,1)} %collective-permute-done.3), kind=kOutput, calls=%fused_computation.75 | convolution fusion | flops 138477568 | bytes 4464640 | tf_op jit(solution)/shard_map/dot_general | solution.py:45
  90.3 2.0 %fusion.39 = bf16[1024,64]{0,1:T(8,128)(2,1)S(1)} fusion(f32[1024,1024]{0,1:T(8,128)S(1)} %copy-done.1, f32[1024]{0:T(1024)S(1)} %fusion, f32[1024]{0:T(1024)S(1)} %get-tuple-element.15, bf16[1024,256]{0,1:T(8,128)(2,1)} %collective-permute-done), kind=kOutput, calls=%fused_computation.81 | convolution fusion | flops 138477568 | bytes 4464640 | tf_op jit(solution)/shard_map/dot_general | solution.py:45
  92.5 1.9 %fusion.38 = bf16[1024,64]{0,1:T(8,128)(2,1)S(1)} fusion(f32[1024,1024]{0,1:T(8,128)S(1)} %copy-done.2, f32[1024]{0:T(1024)S(1)} %fusion.1, f32[1024]{0:T(1024)S(1)} %get-tuple-element.13, bf16[1024,256]{0,1:T(8,128)(2,1)} %collective-permute-done), kind=kOutput, calls=%fused_computation.80 | convolution fusion | flops 138477568 | bytes 4464640 | tf_op jit(solution)/shard_map/dot_general | solution.py:45
  94.8 9.2 %all_to_all.5 = bf16[2,512,128]{1,2,0:T(8,128)(2,1)} all-to-all(bf16[2,512,128]{1,2,0:T(8,128)(2,1)S(1)} %pad_maximum_fusion.1), channel_id=1, replica_groups=mesh['groups'=2,'img'=4,'pair'=2,'sub'=2] {'sub'}, dimensions={0} | all-to-all | bytes 524288 | tf_op jit(solution)/shard_map/all_to_all | solution.py:91
  104.0 1.7 %fusion.183 = (f32[512]{0:T(512)S(1)}, f32[512,512]{0,1:T(8,128)S(1)}) fusion(f32[512]{0:T(512)S(1)} %copy-done.6, f32[512,512]{0,1:T(8,128)S(1)} %fusion.87, bf16[512,512]{1,0:T(8,128)(2,1)} %param.16, bf16[512,256]{0,1:T(8,128)(2,1)} %bitcast.29, bf16[256,256]{1,0:T(8,128)(2,1)} %param.15), kind=kOutput, calls=%fused_computation.247 | convolution fusion | flops 202243584 | bytes 2756608 | tf_op jit(solution)/shard_map/dot_general | solution.py:99
  105.9 3.5 %fusion.27 = bf16[1,512,256]{2,1,0:T(8,128)(2,1)} fusion(bf16[512,256]{1,0:T(8,128)(2,1)S(1)} %copy-done, f32[512,512]{0,1:T(8,128)S(1)} %get-tuple-element.38, f32[512]{0:T(512)S(1)} %copy-done.7, f32[512]{0:T(512)S(1)} %copy-done.8, f32[512]{0:T(512)S(1)} %add_rsqrt_fusion, f32[512]{0:T(512)S(1)} %broadcast_multiply_fusion, f32[256]{0:T(256)S(1)} %copy-done.9, ...), kind=kOutput, calls=%fused_computation.69 | convolution fusion | flops 152829952 | bytes 1844228 | tf_op jit(solution)/shard_map/dot_general | solution.py:106
  (50 shorter events, 18.7 us)
Async XLA Ops:
  0.0 105.9 %copy-start = (bf16[512,256]{1,0:T(8,128)(2,1)S(1)}, bf16[512,256]{1,0:T(8,128)(2,1)}, u32[]{:S(2)}) copy-start(bf16[512,256]{1,0:T(8,128)(2,1)} %param.20) | copy-start | bytes 786436
  2.8 23.0 %collective-permute-start.5 = (bf16[1024,256]{0,1:T(8,128)(2,1)S(1)}, bf16[1024,256]{0,1:T(8,128)(2,1)}, u32[]{:S(2)}, u32[]{:S(2)}) collective-permute-start(bf16[1024,256]{0,1:T(8,128)(2,1)S(1)} %pad_maximum_fusion), channel_id=1, source_target_pairs={{0,2},{2,4},{4,6},{6,8},{8,10},{10,12},{12,14},{1,3},{3,5},{5,7},{... | collective-permute-start | bytes 1572872 | tf_op jit(solution)/shard_map/ppermute | solution.py:15
  5.9 26.8 %collective-permute-start.4 = (bf16[1024,256]{0,1:T(8,128)(2,1)S(1)}, bf16[1024,256]{0,1:T(8,128)(2,1)}, u32[]{:S(2)}, u32[]{:S(2)}) collective-permute-start(bf16[1024,256]{0,1:T(8,128)(2,1)S(1)} %pad_maximum_fusion), channel_id=1, source_target_pairs={{0,4},{2,6},{4,8},{6,10},{8,12},{10,14},{1,5},{3,7},{5,9},{7,11},{... | collective-permute-start | bytes 1572872 | tf_op jit(solution)/shard_map/ppermute | solution.py:15
  9.1 31.8 %collective-permute-start.3 = (bf16[1024,256]{0,1:T(8,128)(2,1)S(1)}, bf16[1024,256]{0,1:T(8,128)(2,1)}, u32[]{:S(2)}, u32[]{:S(2)}) collective-permute-start(bf16[1024,256]{0,1:T(8,128)(2,1)S(1)} %pad_maximum_fusion), channel_id=1, source_target_pairs={{0,6},{2,8},{4,10},{6,12},{8,14},{1,7},{3,9},{5,11},{7,13},{9,15},... | collective-permute-start | bytes 1572872 | tf_op jit(solution)/shard_map/ppermute | solution.py:15
  11.1 34.7 %collective-permute-start.2 = (bf16[1024,256]{0,1:T(8,128)(2,1)S(1)}, bf16[1024,256]{0,1:T(8,128)(2,1)S(1)}, u32[]{:S(2)}, u32[]{:S(2)}) collective-permute-start(bf16[1024,256]{0,1:T(8,128)(2,1)S(1)} %pad_maximum_fusion), channel_id=1, source_target_pairs={{6,0},{8,2},{10,4},{12,6},{14,8},{7,1},{9,3},{11,5},{13,7},{15,9},... | collective-permute-start | bytes 1572872 | tf_op jit(solution)/shard_map/ppermute | solution.py:15
  17.1 32.4 %collective-permute-start.1 = (bf16[1024,256]{0,1:T(8,128)(2,1)S(1)}, bf16[1024,256]{0,1:T(8,128)(2,1)S(1)}, u32[]{:S(2)}, u32[]{:S(2)}) collective-permute-start(bf16[1024,256]{0,1:T(8,128)(2,1)S(1)} %pad_maximum_fusion), channel_id=1, source_target_pairs={{4,0},{6,2},{8,4},{10,6},{12,8},{14,10},{5,1},{7,3},{9,5},{11,7},{... | collective-permute-start | bytes 1572872 | tf_op jit(solution)/shard_map/ppermute | solution.py:15
  25.8 34.9 %collective-permute-start = (bf16[1024,256]{0,1:T(8,128)(2,1)S(1)}, bf16[1024,256]{0,1:T(8,128)(2,1)}, u32[]{:S(2)}, u32[]{:S(2)}) collective-permute-start(bf16[1024,256]{0,1:T(8,128)(2,1)S(1)} %pad_maximum_fusion), channel_id=1, source_target_pairs={{2,0},{4,2},{6,4},{8,6},{10,8},{12,10},{14,12},{3,1},{5,3},{7,5},{... | collective-permute-start | bytes 1572872 | tf_op jit(solution)/shard_map/ppermute | solution.py:15
  45.8 1.6 %copy-start.4 = (bf16[1024,256]{0,1:T(8,128)(2,1)}, bf16[1024,256]{0,1:T(8,128)(2,1)S(1)}, u32[]{:S(2)}) copy-start(bf16[1024,256]{0,1:T(8,128)(2,1)S(1)} %collective-permute-done.2) | copy-start | bytes 1572868
  83.1 1.9 %copy-start.5 = (bf16[1024,256]{0,1:T(8,128)(2,1)S(1)}, bf16[1024,256]{0,1:T(8,128)(2,1)}, u32[]{:S(2)}) copy-start(bf16[1024,256]{0,1:T(8,128)(2,1)} %copy-done.4) | copy-start | bytes 1572868
  88.1 2.2 %copy-start.1 = (f32[1024,1024]{0,1:T(8,128)S(1)}, f32[1024,1024]{0,1:T(8,128)}, u32[]{:S(2)}) copy-start(f32[1024,1024]{0,1:T(8,128)} %get-tuple-element.16) | copy-start | bytes 12582916
  90.3 2.3 %copy-start.2 = (f32[1024,1024]{0,1:T(8,128)S(1)}, f32[1024,1024]{0,1:T(8,128)}, u32[]{:S(2)}) copy-start(f32[1024,1024]{0,1:T(8,128)} %get-tuple-element.14) | copy-start | bytes 12582916
  92.5 11.5 %copy-start.6 = (f32[512]{0:T(512)S(1)}, f32[512]{0:T(512)}, u32[]{:S(2)}) copy-start(f32[512]{0:T(512)} %param.17) | copy-start | bytes 6148
  94.4 11.5 %copy-start.3 = (bf16[1,1024,256]{2,1,0:T(8,128)(2,1)S(1)}, bf16[1,1024,256]{2,1,0:T(8,128)(2,1)}, u32[]{:S(2)}) copy-start(bf16[1,1024,256]{2,1,0:T(8,128)(2,1)} %param.11) | copy-start | bytes 1572868
  94.4 11.5 %copy-start.7 = (f32[512]{0:T(512)S(1)}, f32[512]{0:T(512)}, u32[]{:S(2)}) copy-start(f32[512]{0:T(512)} %param.19) | copy-start | bytes 6148
  94.4 11.5 %copy-start.8 = (f32[512]{0:T(512)S(1)}, f32[512]{0:T(512)}, u32[]{:S(2)}) copy-start(f32[512]{0:T(512)} %param.18) | copy-start | bytes 6148
  94.4 11.5 %copy-start.9 = (f32[256]{0:T(256)S(1)}, f32[256]{0:T(256)}, u32[]{:S(2)}) copy-start(f32[256]{0:T(256)} %param.21) | copy-start | bytes 3076
